TPU v7x, 256 devices: a whole 4x4x8 slice. The times are simulated.
256 devices in a mesh: leaf: 32 (over z, y), head: 8 (over x, core).
Axes of the slice: x: 4, y: 4, z: 8, core: 2. Of those that a mesh axis runs over, the one named last changes fastest.
Arguments:
- query_in: bfloat16 [4096, 8192], P('leaf', 'head'), may hold values from -12 to 12
- key_in: bfloat16 [4096, 1024], P(('leaf', 'head')), may hold values from -12 to 12
- value_in: bfloat16 [4096, 1024], P(('leaf', 'head')), may hold values from -6 to 6
- out_grad: bfloat16 [4096, 8192], P('leaf', 'head'), may hold values from -6 to 6
- ancestry: int32 [32, 8], replicated, may hold values from -1 to 31, as said below
- node_len: int32 [32], replicated, may hold values from 64 to 128, as said below
Outputs:
- attended: bfloat16 [4096, 8192], P('leaf', 'head')
- query_grad: float32 [4096, 8192], P('leaf', 'head')
- key_grad: float32 [4096, 1024], P(('leaf', 'head'))
- value_grad: float32 [4096, 1024], P(('leaf', 'head'))
Inputs may be any that keep to these rules, and one draw needn't show every extreme that they name: `ancestry`: row g lists the ancestors of node g from the root, node 0, at column 0 down to node g itself at column depth(g), then -1; every ancestor of a node comes before it; nodes 0 to 3 form a chain. `node_len`: the root's length is 128, the last node's 128 // 2.
All inputs are finite; a program needn't handle non-finite values.
Results may differ from a plain program's by a relative error of at most 0.019.
Values may be sent and summed in bfloat16 or wider, within the bound.
No kernel may reach another device: no remote copies, remote signals or barrier semaphores. Data moves between devices by JAX's collectives and lax.ppermute only.
A program may use at most 64 MiB of HBM per device.

v0:
```python
import math
import jax
import jax.numpy as jnp
from jax import lax
from jax.sharding import PartitionSpec as P

QH = 64
KVH = 8
HD = 128
BLK = 128
start_level = -1e30
tile_rows = 256


def over_tiles(length, update, carry):
    tile_width = math.gcd(length, tile_rows)
    return lax.fori_loop(
        0,
        length // tile_width,
        lambda number, state: update(state, number * tile_width, tile_width),
        carry,
    )


def token_tags(length_table, first, amount):
    position = first + jnp.arange(amount, dtype=jnp.int32)
    lengths = lax.dynamic_slice_in_dim(length_table, first, amount, 0)
    return (jnp.where(position % BLK < lengths, position // BLK, -2), position)


def visible(ancestor_rows, query_position, key_tag, key_position):
    member = jnp.any(ancestor_rows[:, :, None] == key_tag[None, None, :], axis=1)
    own_node = query_position // BLK
    return member & (
        (key_tag[None, :] != own_node[:, None]) | (key_position[None, :] <= query_position[:, None])
    )


def logits_of(query_group, key_tile, allowed):
    key_count = key_tile.shape[0]
    key_rows = key_tile.reshape(key_count, query_group.shape[1], HD)
    raw = jnp.einsum(
        "tkgd,skd->kgts", query_group, key_rows, preferred_element_type=jnp.float32
    ) * HD ** (-0.5)
    return jnp.where(allowed[None, None], raw, -jnp.inf)


def forward_tile(state, query_group, key_tile, value_tile, allowed):
    row_top, total, accum = state
    logits = logits_of(query_group, key_tile, allowed)
    new_top = jnp.maximum(row_top, jnp.max(logits, axis=-1))
    factor = jnp.exp(row_top - new_top)
    expo = jnp.exp(logits - new_top[..., None])
    total = total * factor + jnp.sum(expo, axis=-1)
    value_rows = value_tile.reshape(value_tile.shape[0], query_group.shape[1], HD)
    accum = accum * factor[..., None] + jnp.einsum(
        "kgts,skd->kgtd", expo.astype(jnp.bfloat16), value_rows, preferred_element_type=jnp.float32
    )
    return (new_top, total, accum)


def gradient_tile(query_group, grad_group, lse, delta, key_tile, value_tile, allowed):
    logits = logits_of(query_group, key_tile, allowed)
    weights = jnp.exp(logits - lse[..., None])
    value_rows = value_tile.reshape(value_tile.shape[0], query_group.shape[1], HD)
    dprob = jnp.einsum("tkgd,skd->kgts", grad_group, value_rows, preferred_element_type=jnp.float32)
    dlogit = (weights * (dprob - delta[..., None])).astype(jnp.bfloat16)
    return (weights.astype(jnp.bfloat16), dlogit)


def per_device(query_in, key_in, value_in, out_grad, ancestry, node_len):
    key_local, value_local = (
        lax.all_to_all(key_in, "head", split_axis=1, concat_axis=0, tiled=True),
        lax.all_to_all(value_in, "head", split_axis=1, concat_axis=0, tiled=True),
    )
    rows = query_in.shape[0]
    key_heads = key_local.shape[1] // HD
    group = QH // KVH
    leaf_base = lax.axis_index("leaf") * rows
    length_table = jnp.repeat(node_len, BLK)
    ancestor_table = jnp.repeat(ancestry, BLK, axis=0)
    all_rows = length_table.shape[0]
    query_position = leaf_base + jnp.arange(rows, dtype=jnp.int32)
    query_ancestors = lax.dynamic_slice_in_dim(ancestor_table, leaf_base, rows, 0)
    query_group = query_in.reshape(rows, key_heads, group, HD)
    grad_group = out_grad.reshape(rows, key_heads, group, HD)
    initial = (
        jnp.full((key_heads, group, rows), start_level, jnp.float32),
        jnp.zeros((key_heads, group, rows), jnp.float32),
        jnp.zeros((key_heads, group, rows, HD), jnp.float32),
    )
    key_piece = lax.all_gather(key_local, "leaf", axis=0, tiled=True)
    value_piece = lax.all_gather(value_local, "leaf", axis=0, tiled=True)

    def update(inner, offset, tile_width):
        key_tile = lax.dynamic_slice_in_dim(key_piece, offset, tile_width, 0)
        value_tile = lax.dynamic_slice_in_dim(value_piece, offset, tile_width, 0)
        key_tag, key_position = token_tags(length_table, offset, tile_width)
        allowed = visible(query_ancestors, query_position, key_tag, key_position)
        return forward_tile(inner, query_group, key_tile, value_tile, allowed)

    row_top, total, accum = over_tiles(key_piece.shape[0], update, initial)
    key_all, value_all = (
        lax.all_gather(key_local, "leaf", axis=0, tiled=True),
        lax.all_gather(value_local, "leaf", axis=0, tiled=True),
    )
    output = (accum / total[..., None]).astype(jnp.bfloat16)
    log_total = row_top + jnp.log(total)
    delta = jnp.sum(
        grad_group.transpose(1, 2, 0, 3).astype(jnp.float32) * output.astype(jnp.float32), axis=-1
    )
    attended = output.transpose(2, 0, 1, 3).reshape(rows, key_heads * group * HD)
    query_zero = jnp.zeros((rows, key_heads, group, HD), jnp.float32)

    def update_both(state, offset, tile_width):
        query_acc, buffer = state
        key_tile = lax.dynamic_slice_in_dim(key_all, offset, tile_width, 0)
        value_tile = lax.dynamic_slice_in_dim(value_all, offset, tile_width, 0)
        key_tag, key_position = token_tags(length_table, offset, tile_width)
        allowed = visible(query_ancestors, query_position, key_tag, key_position)
        probs, dlogit = gradient_tile(
            query_group, grad_group, log_total, delta, key_tile, value_tile, allowed
        )
        key_rows = key_tile.reshape(tile_width, key_heads, HD)
        query_acc = query_acc + jnp.einsum(
            "kgts,skd->tkgd", dlogit, key_rows, preferred_element_type=jnp.float32
        )
        key_term = jnp.einsum(
            "kgts,tkgd->skd", dlogit, query_group, preferred_element_type=jnp.float32
        )
        value_term = jnp.einsum(
            "kgts,tkgd->skd", probs, grad_group, preferred_element_type=jnp.float32
        )
        both_terms = jnp.concatenate(
            [
                key_term.reshape(tile_width, key_heads * HD),
                value_term.reshape(tile_width, key_heads * HD),
            ],
            axis=1,
        )
        buffer = lax.dynamic_update_slice_in_dim(buffer, both_terms, offset, 0)
        return (query_acc, buffer)

    buffer_zero = jnp.zeros((all_rows, 2 * key_heads * HD), jnp.float32)
    query_sum, buffer = over_tiles(all_rows, update_both, (query_zero, buffer_zero))
    summed = lax.psum_scatter(
        buffer.astype(jnp.bfloat16), "leaf", scatter_dimension=0, tiled=True
    ).astype(jnp.float32)
    key_sum = summed[:, : key_heads * HD]
    value_grad = summed[:, key_heads * HD :]
    scale = HD ** (-0.5)
    query_grad = (query_sum * scale).reshape(rows, key_heads * group * HD)
    key_grad = key_sum * scale
    key_grad, value_grad = (
        lax.all_to_all(
            key_grad.astype(jnp.bfloat16), "head", split_axis=0, concat_axis=1, tiled=True
        ).astype(key_grad.dtype),
        lax.all_to_all(
            value_grad.astype(jnp.bfloat16), "head", split_axis=0, concat_axis=1, tiled=True
        ).astype(value_grad.dtype),
    )
    return (attended, query_grad, key_grad, value_grad)


def solution(mesh):
    return jax.shard_map(
        per_device,
        mesh=mesh,
        in_specs=(
            P("leaf", "head"),
            P(("leaf", "head"), None),
            P(("leaf", "head"), None),
            P("leaf", "head"),
            P(),
            P(),
        ),
        out_specs=(
            P("leaf", "head"),
            P("leaf", "head"),
            P(("leaf", "head"), None),
            P(("leaf", "head"), None),
        ),
        check_vma=False,
    )
```

profile of v0, /device:TPU:1, one launch (start us, length us, event | category | flops | bytes accessed | tf_op | source)
XLA Modules:
  0.0 555.6 jit_solution(12811123765744551282)
XLA Ops:
  7.9 11.0 %all_to_all.64 = bf16[16,8,128]{2,0,1:T(8,128)(2,1)} all-to-all(bf16[16,8,128]{2,0,1:T(8,128)(2,1)S(1)} %copy_bitcast_fusion.3), channel_id=1, replica_groups=mesh['leaf'=32,'head'=8] {'head'}, dimensions={1} | all-to-all | bytes 65536 | tf_op jit(solution)/shard_map/all_to_all | solution.py:73
  19.7 8.5 %all_to_all.65 = bf16[16,8,128]{2,0,1:T(8,128)(2,1)} all-to-all(bf16[16,8,128]{2,0,1:T(8,128)(2,1)S(1)} %copy_bitcast_fusion.2), channel_id=1, replica_groups=mesh['leaf'=32,'head'=8] {'head'}, dimensions={1} | all-to-all | bytes 65536 | tf_op jit(solution)/shard_map/all_to_all | solution.py:74
  31.8 59.2 %all-gather.3.cloned.1.call-done = bf16[4096,128]{1,0:T(8,128)(2,1)} async-done(((bf16[128,128]{1,0:T(8,128)(2,1)}), bf16[4096,128]{1,0:T(8,128)(2,1)}) %all-gather.3.cloned.1.call-update) | async-done | bytes 1048592 | tf_op jit(solution)/shard_map/all_gather | solution.py:92
  91.0 76.5 %all-gather.5.cloned.1.call-done = bf16[4096,128]{1,0:T(8,128)(2,1)} async-done(((bf16[128,128]{1,0:T(8,128)(2,1)}), bf16[4096,128]{1,0:T(8,128)(2,1)}) %all-gather.5.cloned.1.call-update) | async-done | bytes 1048592 | tf_op jit(solution)/shard_map/all_gather | solution.py:93
  167.5 56.2 %while.44 = (s32[]{:T(128)}, f32[1,8,128]{2,1,0:T(8,128)S(1)}, f32[1,8,128]{2,1,0:T(8,128)S(1)}, f32[1,8,128,128]{3,2,1,0:T(8,128)S(1)}, s32[128,8]{1,0:T(8,128)...) while((s32[]{:T(128)}, f32[1,8,128]{2,1,0:T(8,128)S(1)}, ...), condition=%wide.region_4.5_spmd.clone.clone.clone, body=%wide.region_0.4_spmd.clone.clone.clone.sunk | while | flops 137082496 | bytes 4862171 | solution.py:17
  169.6 1.4 fusion.87
  173.1 1.4 fusion.87
  176.6 1.4 fusion.87
  180.1 1.4 fusion.87
  183.6 1.4 fusion.87
  187.1 1.4 fusion.87
  190.7 1.4 fusion.87
  194.2 1.4 fusion.87
  197.7 1.4 fusion.87
  201.2 1.4 fusion.87
  204.7 1.4 fusion.87
  208.2 1.4 fusion.87
  224.8 81.0 %while.45 = (s32[]{:T(128)}, f32[128,1,8,128]{0,3,2,1:T(8,128)S(1)}, bf16[4096,256]{1,0:T(8,128)(2,1)S(1)}, bf16[4096,128]{1,0:T(8,128)(2,1)}, s32[128,8]{1,0:T(...) while((s32[]{:T(128)}, ...), condition=%wide.region_8.9_spmd.clone.clone.clone, body=%wide.region_6.8_spmd.clone.clone.clone.sunk | while | flops 338534016 | bytes 8147185 | solution.py:17
  307.2 216.1 %reduce-scatter.2.cloned.1.call-done = bf16[128,256]{1,0:T(8,128)(2,1)} async-done(((bf16[4096,256]{1,0:T(8,128)(2,1)}), bf16[128,256]{1,0:T(8,128)(2,1)}) %reduce-scatter.2.cloned.1.call-update) | async-done | bytes 65552 | tf_op jit(solution)/shard_map/reduce_scatter | solution.py:146
  523.3 1.5 multiply_convert_fusion
  524.8 10.3 %all-to-all-start.2 = ((bf16[8,16,128]{2,1,0:T(8,128)(2,1)}), bf16[8,16,128]{2,1,0:T(8,128)(2,1)S(1)}, u32[]{:S(2)}, u32[]{:S(2)}) async-start(bf16[8,16,128]{2,1,0:T(8,128)(2,1)} %bitcast.14), calls=%async_computation.3 | async-start | bytes 65536 | tf_op jit(solution)/shard_map/all_to_all | solution.py:155
  537.6 2.2 all-to-all-done.2
  539.8 4.0 all-to-all-start.3
  544.4 4.1 all-to-all-done.3
  (411 shorter events, 128.9 us)
Async XLA Ops:
  7.2 0.8 copy-start
  7.2 24.5 %copy-start.4 = (s32[32]{0:T(128)S(1)}, s32[32]{0:T(128)}, u32[]{:S(2)}) copy-start(s32[32]{0:T(128)} %param.15) | copy-start | bytes 388
  7.2 83.8 %all-gather.3.cloned.1.call-start = ((), (), s32[]{:S(2)}) async-start(), calls=%async_computation.5 | async-start | bytes 1081344 | tf_op jit(solution)/shard_map/all_gather | solution.py:92
  18.9 148.6 %all-gather.5.cloned.1.call-start = ((), (), s32[]{:S(2)}) async-start(), calls=%async_computation.6 | async-start | bytes 1081344 | tf_op jit(solution)/shard_map/all_gather | solution.py:93
  28.2 495.1 %reduce-scatter.2.cloned.1.call-start = ((), (), s32[]{:S(2)}) async-start(), calls=%async_computation.7 | async-start | bytes 2162688 | tf_op jit(solution)/shard_map/reduce_scatter | solution.py:146
  305.8 1.3 copy-start.1
  305.8 229.3 %copy-start.2 = (bf16[1,8,128,128]{2,3,1,0:T(8,128)(2,1)S(1)}, bf16[1,8,128,128]{2,3,1,0:T(8,128)(2,1)}, u32[]{:S(2)}) copy-start(bf16[1,8,128,128]{2,3,1,0:T(8,128)(2,1)} %get-tuple-element.949) | copy-start | bytes 786436
  523.3 13.6 %copy-start.3 = (bf16[128,256]{1,0:T(8,128)(2,1)S(1)}, bf16[128,256]{1,0:T(8,128)(2,1)}, u32[]{:S(2)}) copy-start(bf16[128,256]{1,0:T(8,128)(2,1)} %reduce-scatter.2.cloned.1.call-done) | copy-start | bytes 196612
  524.8 15.0 %all-to-all-start.2 = ((bf16[8,16,128]{2,1,0:T(8,128)(2,1)}), bf16[8,16,128]{2,1,0:T(8,128)(2,1)S(1)}, u32[]{:S(2)}, u32[]{:S(2)}) async-start(bf16[8,16,128]{2,1,0:T(8,128)(2,1)} %bitcast.14), calls=%async_computation.3 | async-start | bytes 65536 | tf_op jit(solution)/shard_map/all_to_all | solution.py:155
  539.8 8.7 %all-to-all-start.3 = ((bf16[8,16,128]{2,1,0:T(8,128)(2,1)}), bf16[8,16,128]{2,1,0:T(8,128)(2,1)S(1)}, u32[]{:S(2)}, u32[]{:S(2)}) async-start(bf16[8,16,128]{2,1,0:T(8,128)(2,1)} %bitcast.16), calls=%async_computation.4 | async-start | bytes 65536 | tf_op jit(solution)/shard_map/all_to_all | solution.py:158
Sparse Core Ops, SparseCore 0:
  19.0 71.9 all-gather.2
  93.6 73.8 all-gather.4
  307.3 215.9 reduce-scatter.1
where the time goes:
time: 560 us; the launch traced here: 556 us
  waiting for transfers between devices  358 us (64%)
  matrix products  106 us (19%)
  other arithmetic  25.9 us (5%)
  blocking collectives  19.4 us (3%)
  local copies, waits for them, and re-layouts  14.7 us (3%)
  starting transfers between devices  14.4 us (3%)
  between operations  13.9 us (2%)
    reduce_scatter x1, waiting for transfers between devices, per_device(): lax.psum_scatter(buffer.astype(jnp.bfloat16), 'leaf', scatter_dimension=0...  216 us
    all_gather x1, waiting for transfers between devices, per_device(): value_piece = lax.all_gather(value_local, 'leaf', axis=0, tiled=True)  76.5 us
    all_gather x1, waiting for transfers between devices, per_device(): key_piece = lax.all_gather(key_local, 'leaf', axis=0, tiled=True)  59.2 us
    dot_general x32, matrix products, logits_of(): jnp.einsum('tkgd,skd->kgts', query_group, key_rows, preferred_element_typ...  37.6 us
    dot_general x16, matrix products, forward_tile(): jnp.einsum('kgts,skd->kgtd', expo.astype(jnp.bfloat16), value_rows, prefe...  21.8 us
    dot_general x16, matrix products, update_both(): jnp.einsum('kgts,skd->tkgd', dlogit, key_rows, preferred_element_type=jnp...  18.5 us
    dot_general x16, matrix products, gradient_tile(): jnp.einsum('tkgd,skd->kgts', grad_group, value_rows, preferred_element_ty...  18.1 us
    reduce_or x32, other arithmetic, visible(): jnp.any(ancestor_rows[:, :, None] == key_tag[None, None, :], axis=1)  13 us
  transfers between devices with their start and end apart: 5, of which 5 were waited for; matrix products, arithmetic and copies ran while one was open for 1% of the time, Pallas kernels for 0%

commit v1 on v0

--- a/solution.py
+++ b/solution.py
@@ -90,7 +90,10 @@
         jnp.zeros((key_heads, group, rows, HD), jnp.float32),
     )
     key_piece = lax.all_gather(key_local, "leaf", axis=0, tiled=True)
-    value_piece = lax.all_gather(value_local, "leaf", axis=0, tiled=True)
+    size = lax.axis_size("leaf")
+    pieces = jnp.stack([value_local for _ in range(size)])
+    pieces = lax.all_to_all(pieces, "leaf", split_axis=0, concat_axis=0)
+    value_piece = jnp.concatenate(pieces, axis=0)
 
     def update(inner, offset, tile_width):
         key_tile = lax.dynamic_slice_in_dim(key_piece, offset, tile_width, 0)

time: 560 us -> 514 us (0.918)
  waiting for transfers between devices: 358 us -> 325 us
  starting transfers between devices: 14.4 us -> 35.3 us
  blocking collectives: 19.4 us -> 0 us
  matrix products: 106 us -> 92.5 us
    all_gather x1, waiting for transfers between devices: 76.5 us -> 33.3 us  [per_device(): lax.all_gather(value_local, 'leaf', axis=0, tiled=True)]
    all_to_all x0 -> x3, starting transfers between devices: none -> 21 us  [the longest x1 10.5 us: per_device(): pieces = lax.all_to_all(pieces, 'leaf', split_axis=0, concat_axis=0)]
    all_to_all x2 -> x0, blocking collectives: 19.4 us -> none  [the longest x1 11 us: per_device(): lax.all_to_all(key_in, 'head', split_axis=1, concat_axis=0, tiled=True)]
    dot_general x16, matrix products: 21.8 us -> 8.41 us  [forward_tile(): jnp.einsum('kgts,skd->kgtd', expo.astype(jnp.bfloat16), value_rows, prefe...]
    all_to_all x0 -> x3, waiting for transfers between devices: none -> 7.38 us  [the longest x1 4.02 us: per_device(): lax.all_to_all(value_in, 'head', split_axis=1, concat_axis=0, tiled=True)]
  transfers between devices with their start and end apart: 5 -> 8, of which waited for: 5 -> 7; matrix products, arithmetic and copies ran while one was open for 1% -> 10% of each run, Pallas kernels for 0% -> 0%
where the time goes in v1:
time: 514 us; the launch traced here: 510 us
  waiting for transfers between devices  325 us (63%)
  matrix products  92.5 us (18%)
  starting transfers between devices  35.3 us (7%)
  other arithmetic  25.9 us (5%)
  local copies, waits for them, and re-layouts  14.7 us (3%)
  between operations  14 us (3%)
    reduce_scatter x1, waiting for transfers between devices, per_device(): lax.psum_scatter(buffer.astype(jnp.bfloat16), 'leaf', scatter_dimension=0...  216 us
    all_gather x1, waiting for transfers between devices, per_device(): key_piece = lax.all_gather(key_local, 'leaf', axis=0, tiled=True)  61.1 us
    dot_general x32, matrix products, logits_of(): jnp.einsum('tkgd,skd->kgts', query_group, key_rows, preferred_element_typ...  37.6 us
    all_gather x1, waiting for transfers between devices, per_device(): lax.all_gather(value_local, 'leaf', axis=0, tiled=True)  33.3 us
    dot_general x16, matrix products, update_both(): jnp.einsum('kgts,skd->tkgd', dlogit, key_rows, preferred_element_type=jnp...  18.5 us
    dot_general x16, matrix products, gradient_tile(): jnp.einsum('tkgd,skd->kgts', grad_group, value_rows, preferred_element_ty...  18.1 us
    reduce_or x32, other arithmetic, visible(): jnp.any(ancestor_rows[:, :, None] == key_tag[None, None, :], axis=1)  13 us
    all_to_all x1, starting transfers between devices, per_device(): pieces = lax.all_to_all(pieces, 'leaf', split_axis=0, concat_axis=0)  10.5 us
  transfers between devices with their start and end apart: 8, of which 7 were waited for; matrix products, arithmetic and copies ran while one was open for 10% of the time, Pallas kernels for 0%

profile of v1, /device:TPU:1, one launch (start us, length us, event | category | flops | bytes accessed | tf_op | source)
XLA Modules:
  0.0 510.5 jit_solution(13447978047050331390)
XLA Ops:
  8.6 6.4 %all-to-all-start = ((bf16[16,8,128]{2,0,1:T(8,128)(2,1)}), bf16[16,8,128]{2,0,1:T(8,128)(2,1)S(1)}, u32[]{:S(2)}, u32[]{:S(2)}) async-start(bf16[16,8,128]{2,0,1:T(8,128)(2,1)} %copy_bitcast_fusion.3), calls=%async_computation | async-start | bytes 65536 | tf_op jit(solution)/shard_map/all_to_all | solution.py:73
  15.0 1.4 copy_bitcast_fusion.2
  16.4 3.4 all-to-all-done
  19.7 4.0 all-to-all-start.1
  24.4 4.0 all-to-all-done.1
  28.5 1.2 stack.5
  29.7 10.5 %all-to-all-start.2 = ((bf16[32,128,128]{2,1,0:T(8,128)(2,1)}), bf16[32,128,128]{2,1,0:T(8,128)(2,1)S(1)}, u32[]{:S(2)}, u32[]{:S(2)}) async-start(bf16[32,128,128]{2,1,0:T(8,128)(2,1)} %stack.5), calls=%async_computation.2 | async-start | bytes 2097152 | tf_op jit(solution)/shard_map/all_to_all | solution.py:95
  41.3 61.1 %all-gather.3.cloned.1.call-done = bf16[4096,128]{1,0:T(8,128)(2,1)} async-done(((bf16[128,128]{1,0:T(8,128)(2,1)}), bf16[4096,128]{1,0:T(8,128)(2,1)}) %all-gather.3.cloned.1.call-update) | async-done | bytes 1048592 | tf_op jit(solution)/shard_map/all_gather | solution.py:92
  102.4 42.8 %while.44 = (s32[]{:T(128)}, f32[1,8,128]{2,1,0:T(8,128)S(1)}, f32[1,8,128]{2,1,0:T(8,128)S(1)}, f32[1,8,128,128]{3,2,1,0:T(8,128)S(1)}, s32[128,8]{1,0:T(8,128)...) while((s32[]{:T(128)}, f32[1,8,128]{2,1,0:T(8,128)S(1)}, ...), condition=%wide.region_4.5_spmd.clone.clone.clone, body=%wide.region_0.4_spmd.clone.clone.clone.sunk | while | flops 137082496 | bytes 4862171 | solution.py:17
  146.2 33.3 %all-gather.5.cloned.1.call-done = bf16[4096,128]{1,0:T(8,128)(2,1)} async-done(((bf16[128,128]{1,0:T(8,128)(2,1)}), bf16[4096,128]{1,0:T(8,128)(2,1)}) %all-gather.5.cloned.1.call-update) | async-done | bytes 1048592 | tf_op jit(solution)/shard_map/all_gather | solution.py:108
  179.7 81.0 %while.45 = (s32[]{:T(128)}, f32[128,1,8,128]{0,3,2,1:T(8,128)S(1)}, bf16[4096,256]{1,0:T(8,128)(2,1)S(1)}, bf16[4096,128]{1,0:T(8,128)(2,1)}, s32[128,8]{1,0:T(...) while((s32[]{:T(128)}, ...), condition=%wide.region_8.9_spmd.clone.clone.clone, body=%wide.region_6.8_spmd.clone.clone.clone.sunk | while | flops 338534016 | bytes 8147185 | solution.py:17
  195.6 1.2 fusion.99
  200.7 1.2 fusion.99
  210.8 1.2 fusion.99
  220.9 1.2 fusion.99
  226.0 1.2 fusion.99
  236.1 1.2 fusion.99
  260.7 1.3 copy-done.1
  262.0 216.1 %reduce-scatter.2.cloned.1.call-done = bf16[128,256]{1,0:T(8,128)(2,1)} async-done(((bf16[4096,256]{1,0:T(8,128)(2,1)}), bf16[128,256]{1,0:T(8,128)(2,1)}) %reduce-scatter.2.cloned.1.call-update) | async-done | bytes 65552 | tf_op jit(solution)/shard_map/reduce_scatter | solution.py:149
  478.1 1.5 multiply_convert_fusion
  479.6 10.3 %all-to-all-start.3 = ((bf16[8,16,128]{2,1,0:T(8,128)(2,1)}), bf16[8,16,128]{2,1,0:T(8,128)(2,1)S(1)}, u32[]{:S(2)}, u32[]{:S(2)}) async-start(bf16[8,16,128]{2,1,0:T(8,128)(2,1)} %bitcast.16), calls=%async_computation.4 | async-start | bytes 65536 | tf_op jit(solution)/shard_map/all_to_all | solution.py:158
  492.4 2.2 all-to-all-done.3
  494.6 4.0 all-to-all-start.4
  499.2 4.1 all-to-all-done.4
  (426 shorter events, 121.4 us)
Async XLA Ops:
  7.2 0.8 copy-start
  7.2 33.1 %copy-start.8 = (s32[32,8]{0,1:T(8,128)S(1)}, s32[32,8]{0,1:T(8,128)}, u32[]{:S(2)}) copy-start(s32[32,8]{0,1:T(8,128)} %param.14) | copy-start | bytes 3076
  7.2 33.2 %copy-start.4 = (bf16[128,1024]{1,0:T(8,128)(2,1)S(1)}, bf16[128,1024]{1,0:T(8,128)(2,1)}, u32[]{:S(2)}) copy-start(bf16[128,1024]{1,0:T(8,128)(2,1)} %param.10) | copy-start | bytes 786436
  8.6 11.2 %all-to-all-start = ((bf16[16,8,128]{2,0,1:T(8,128)(2,1)}), bf16[16,8,128]{2,0,1:T(8,128)(2,1)S(1)}, u32[]{:S(2)}, u32[]{:S(2)}) async-start(bf16[16,8,128]{2,0,1:T(8,128)(2,1)} %copy_bitcast_fusion.3), calls=%async_computation | async-start | bytes 65536 | tf_op jit(solution)/shard_map/all_to_all | solution.py:73
  19.7 4.0 copy-start.6
  19.7 8.7 %all-to-all-start.1 = ((bf16[16,8,128]{2,0,1:T(8,128)(2,1)}), bf16[16,8,128]{2,0,1:T(8,128)(2,1)S(1)}, u32[]{:S(2)}, u32[]{:S(2)}) async-start(bf16[16,8,128]{2,0,1:T(8,128)(2,1)} %copy_bitcast_fusion.2), calls=%async_computation.1 | async-start | bytes 65536 | tf_op jit(solution)/shard_map/all_to_all | solution.py:74
  23.7 78.7 %all-gather.3.cloned.1.call-start = ((), (), s32[]{:S(2)}) async-start(), calls=%async_computation.6 | async-start | bytes 1081344 | tf_op jit(solution)/shard_map/all_gather | solution.py:92
  28.5 12.3 %copy-start.3 = (bf16[16,8,128]{2,0,1:T(8,128)(2,1)}, bf16[16,8,128]{2,0,1:T(8,128)(2,1)S(1)}, u32[]{:S(2)}) copy-start(bf16[16,8,128]{2,0,1:T(8,128)(2,1)S(1)} %all-to-all-done.1) | copy-start | bytes 98308
  28.5 12.3 %copy-start.5 = (bf16[128,1024]{1,0:T(8,128)(2,1)S(1)}, bf16[128,1024]{1,0:T(8,128)(2,1)}, u32[]{:S(2)}) copy-start(bf16[128,1024]{1,0:T(8,128)(2,1)} %param.13) | copy-start | bytes 786436
  29.7 72.7 %all-to-all-start.2 = ((bf16[32,128,128]{2,1,0:T(8,128)(2,1)}), bf16[32,128,128]{2,1,0:T(8,128)(2,1)S(1)}, u32[]{:S(2)}, u32[]{:S(2)}) async-start(bf16[32,128,128]{2,1,0:T(8,128)(2,1)} %stack.5), calls=%async_computation.2 | async-start | bytes 2097152 | tf_op jit(solution)/shard_map/all_to_all | solution.py:95
  40.2 0.9 copy-start.9
  40.2 139.3 %all-gather.5.cloned.1.call-start = ((), (), s32[]{:S(2)}) async-start(), calls=%async_computation.7 | async-start | bytes 1081344 | tf_op jit(solution)/shard_map/all_gather | solution.py:108
  41.2 436.9 %reduce-scatter.2.cloned.1.call-start = ((), (), s32[]{:S(2)}) async-start(), calls=%async_computation.8 | async-start | bytes 2162688 | tf_op jit(solution)/shard_map/reduce_scatter | solution.py:149
  260.6 1.3 copy-start.1
  260.6 229.3 %copy-start.2 = (bf16[1,8,128,128]{2,3,1,0:T(8,128)(2,1)S(1)}, bf16[1,8,128,128]{2,3,1,0:T(8,128)(2,1)}, u32[]{:S(2)}) copy-start(bf16[1,8,128,128]{2,3,1,0:T(8,128)(2,1)} %get-tuple-element.949) | copy-start | bytes 786436
  478.1 13.6 %copy-start.7 = (bf16[128,256]{1,0:T(8,128)(2,1)S(1)}, bf16[128,256]{1,0:T(8,128)(2,1)}, u32[]{:S(2)}) copy-start(bf16[128,256]{1,0:T(8,128)(2,1)} %reduce-scatter.2.cloned.1.call-done) | copy-start | bytes 196612
  479.6 15.0 %all-to-all-start.3 = ((bf16[8,16,128]{2,1,0:T(8,128)(2,1)}), bf16[8,16,128]{2,1,0:T(8,128)(2,1)S(1)}, u32[]{:S(2)}, u32[]{:S(2)}) async-start(bf16[8,16,128]{2,1,0:T(8,128)(2,1)} %bitcast.16), calls=%async_computation.4 | async-start | bytes 65536 | tf_op jit(solution)/shard_map/all_to_all | solution.py:158
  494.6 8.7 %all-to-all-start.4 = ((bf16[8,16,128]{2,1,0:T(8,128)(2,1)}), bf16[8,16,128]{2,1,0:T(8,128)(2,1)S(1)}, u32[]{:S(2)}, u32[]{:S(2)}) async-start(bf16[8,16,128]{2,1,0:T(8,128)(2,1)} %bitcast.18), calls=%async_computation.5 | async-start | bytes 65536 | tf_op jit(solution)/shard_map/all_to_all | solution.py:161
Sparse Core Ops, SparseCore 0:
  27.7 74.6 all-gather.2
  105.6 73.9 all-gather.4
  262.1 215.9 reduce-scatter.1
